TPU v7x, 256 devices: a whole 4x4x8 slice. The times are simulated.
256 devices in a mesh: src: 16 (over x_lo, y, core), rcv: 16 (over z, x_hi).
Axes of the slice: x: 4 (x_hi: 2, x_lo: 2; x = x_hi * 2 + x_lo), y: 4, z: 8, core: 2. Of those that a mesh axis runs over, the one named last changes fastest.
Arguments:
- recorded: bfloat16 [2, 16384, 16384], P(None, 'src', 'rcv'), may hold values from -6 to 6
- obliquity: float32 [16, 1024], replicated, may hold values from 0.01 to 0.25
- clip_level: float32 [16384], P('src'), may hold values from 0.3 to 3
Outputs:
- first_pass: bfloat16 [2, 16384, 16384], P(None, 'src', 'rcv')
- primaries: bfloat16 [2, 16384, 16384], P(None, 'src', 'rcv')
All inputs are finite; a program needn't handle non-finite values.
Results may differ from a plain program's by a relative error of at most 0.0025.
Values may be sent and summed in bfloat16 or wider, within the bound.
A program may use at most 128 MiB of HBM per device.

v0:
```python
import math
import jax
import jax.numpy as jnp
from jax import lax
from jax.sharding import PartitionSpec as P

N = 16384
K = 256
TWO_PI = 2.0 * math.pi


def rotate(real_part, imag_part, cosine, sine_part):
    return (real_part * cosine - imag_part * sine_part, real_part * sine_part + imag_part * cosine)


def twiddle(real_part, imag_part, column_index, group_index, orient, total_length):
    angles = (column_index * group_index % total_length).astype(jnp.float32) * (
        TWO_PI / total_length
    )
    return rotate(real_part, imag_part, jnp.cos(angles), orient * jnp.sin(angles))


def long_table(length, orient):
    index_left = lax.broadcasted_iota(jnp.int32, (length, length), 0)
    index_right = lax.broadcasted_iota(jnp.int32, (length, length), 1)
    angles = (index_left * index_right % length).astype(jnp.float32) * (TWO_PI / length)
    cosine = jnp.cos(angles)
    sine_part = orient * jnp.sin(angles)
    upper = jnp.concatenate([cosine, sine_part], axis=1)
    lower = jnp.concatenate([-sine_part, cosine], axis=1)
    return jnp.concatenate([upper, lower], axis=0)


def long_transform(real_part, imag_part, orient):
    length = real_part.shape[-1]
    joined = jnp.concatenate([real_part, imag_part], axis=-1)
    result = jnp.dot(
        joined.reshape(-1, 2 * length),
        long_table(length, orient),
        precision=lax.Precision.HIGHEST,
        preferred_element_type=jnp.float32,
    )
    result = result.reshape(joined.shape)
    return (result[..., :length], result[..., length:])


def across_groups(real_part, imag_part, groups, orient):
    index_left = lax.broadcasted_iota(jnp.int32, (groups, groups), 0)
    index_right = lax.broadcasted_iota(jnp.int32, (groups, groups), 1)
    angles = (index_left * index_right % groups).astype(jnp.float32) * (TWO_PI / groups)
    cosine = jnp.cos(angles)
    sine_part = orient * jnp.sin(angles)
    highest = lax.Precision.HIGHEST
    new_real = jnp.einsum("mgc,gk->mkc", real_part, cosine, precision=highest) - jnp.einsum(
        "mgc,gk->mkc", imag_part, sine_part, precision=highest
    )
    new_imag = jnp.einsum("mgc,gk->mkc", real_part, sine_part, precision=highest) + jnp.einsum(
        "mgc,gk->mkc", imag_part, cosine, precision=highest
    )
    return (new_real, new_imag)


def filter_rows(whole_rows, obliquity, groups):
    row_total = whole_rows.shape[1]
    group_cols = whole_rows.shape[2] // groups
    total_length = groups * group_cols
    values = whole_rows.astype(jnp.float32).reshape(2, row_total, groups, group_cols)
    real_part, imag_part = across_groups(values[0], values[1], groups, -1.0)
    column_index = lax.broadcasted_iota(jnp.int32, (1, 1, group_cols), 2)
    group_index = lax.broadcasted_iota(jnp.int32, (1, groups, 1), 1)
    real_part, imag_part = twiddle(
        real_part, imag_part, column_index, group_index, -1.0, total_length
    )
    real_part, imag_part = long_transform(real_part, imag_part, -1.0)
    real_part = real_part * obliquity[None]
    imag_part = imag_part * obliquity[None]
    real_part, imag_part = long_transform(real_part, imag_part, 1.0)
    real_part, imag_part = twiddle(
        real_part, imag_part, column_index, group_index, 1.0, total_length
    )
    real_part, imag_part = across_groups(real_part, imag_part, groups, 1.0)
    inverse_scale = 1.0 / total_length
    returned = jnp.stack([real_part * inverse_scale, imag_part * inverse_scale])
    return returned.reshape(2, row_total, total_length).astype(jnp.bfloat16)


def through_rows(panel_rows, obliquity):
    moved_rows = lax.all_to_all(panel_rows, "rcv", split_axis=1, concat_axis=2, tiled=True)
    returned = filter_rows(moved_rows, obliquity, lax.axis_size("rcv"))
    return lax.all_to_all(returned, "rcv", split_axis=2, concat_axis=1, tiled=True)


def complex_product(left_rows, right_rows):
    left_joined = jnp.concatenate([left_rows[0], left_rows[1]], axis=0)
    upper = jnp.concatenate([right_rows[0], right_rows[1]], axis=1)
    lower = jnp.concatenate([-right_rows[1], right_rows[0]], axis=1)
    right_joined = jnp.concatenate([upper, lower], axis=0)
    return lax.dot_general(
        left_joined, right_joined, (((0,), (0,)), ((), ())), preferred_element_type=jnp.float32
    )


def per_device(recorded, obliquity, clip_level):
    spacing = N // K
    row_total = recorded.shape[1]
    col_total = recorded.shape[2]
    panel_rows = recorded.reshape(2, row_total // spacing, spacing, col_total)[:, :, 0, :]
    filtered = through_rows(panel_rows, obliquity)
    clip_rows = clip_level[:, None]
    estimate = recorded
    passes = []
    for update_index in range(2):
        columns = estimate.reshape(2, row_total, col_total // spacing, spacing)[:, :, :, 0]
        left_local = jnp.swapaxes(columns, 1, 2)
        left_panel = lax.all_gather(left_local, "rcv", axis=1, tiled=True)

        def accumulate(running, panel_piece, first_row, left_all=left_panel):
            return complex_product(left_all, panel_piece)

        zeros_init = jnp.zeros((row_total, 2 * col_total), jnp.float32)
        product_sum = accumulate(
            zeros_init, lax.all_gather(filtered, "src", axis=1, tiled=True), jnp.int32(0)
        )
        pred_real = product_sum[:, :col_total]
        pred_imag = product_sum[:, col_total:]
        limiter = lax.rsqrt(
            1.0 + (pred_real * pred_real + pred_imag * pred_imag) / (clip_rows * clip_rows)
        )
        estimate = (
            recorded.astype(jnp.float32) - jnp.stack([pred_real * limiter, pred_imag * limiter])
        ).astype(jnp.bfloat16)
        passes.append(estimate)
    return (passes[0], passes[1])


def solution(mesh):
    return jax.shard_map(
        per_device,
        mesh=mesh,
        in_specs=(P(None, "src", "rcv"), P(), P("src")),
        out_specs=(P(None, "src", "rcv"), P(None, "src", "rcv")),
        check_vma=False,
    )
```

profile of v0, /device:TPU:8, one launch (start us, length us, event | category | flops | bytes accessed | tf_op | source)
XLA Modules:
  0.0 447.1 jit_solution(7777668069207956827)
XLA Ops:
  7.2 1.1 slice.88
  8.3 0.7 copy.65
  9.0 11.0 %all-to-all-start = ((bf16[2,16,1024]{2,0,1:T(2,128)(2,1)}), bf16[2,16,1024]{2,0,1:T(2,128)(2,1)S(1)}, u32[]{:S(2)}, u32[]{:S(2)}) async-start(bf16[2,16,1024]{2,0,1:T(2,128)(2,1)} %bitcast.83), calls=%async_computation | async-start | bytes 131072 | tf_op jit(solution)/shard_map/all_to_all | solution.py:88
  20.1 0.0 all-gather.4.cloned.1.call-start
  20.1 6.2 %copy.36 = bf16[2,1024,1024]{1,2,0:T(8,128)(2,1)} copy(bf16[2,1024,1024]{2,1,0:T(8,128)(2,1)} %param.3) | data formatting | bytes 8388608 | tf_op args[0]
  26.3 1.1 slice.85
  27.4 0.7 copy.64
  28.1 0.0 all-gather.6.cloned.1.call-start
  28.2 17.6 %broadcast_multiply_fusion = (f32[1024,1024]{1,0:T(8,128)}, f32[1024,1024]{1,0:T(8,128)}) fusion(), kind=kLoop, calls=%fused_computation.35 | loop fusion | flops 15728640 | bytes 8388608 | tf_op jit(solution)/shard_map/mul | solution.py:28
  45.8 16.3 %fusion.27 = f32[1024,1024]{1,0:T(8,128)} fusion(), kind=kLoop, calls=%fused_computation.39 | loop fusion | flops 16777216 | bytes 4194304 | tf_op jit(solution)/shard_map/neg | solution.py:30
  62.1 16.7 %fusion.24 = (f32[1024,1024]{1,0:T(8,128)}, f32[1024,1024]{1,0:T(8,128)}) fusion(), kind=kLoop, calls=%fused_computation.36 | loop fusion | flops 15728640 | bytes 8388608 | tf_op jit(solution)/shard_map/sin | solution.py:28
  78.9 0.1 fusion.138
  79.0 0.3 fusion.65
  79.2 0.3 fusion.66
  79.5 0.3 convolution_add_fusion.1
  79.8 0.5 subtract_bitcast_fusion
  80.3 13.8 %fusion.21 = f32[1,16,2048]{2,1,0:T(8,128)S(1)} fusion(f32[1024,1024]{1,0:T(8,128)} %get-tuple-element.19, f32[1024,1024]{1,0:T(8,128)} %fusion.27, f32[1024,1024]{1,0:T(8,128)} %get-tuple-element.18, f32[1,16,1024]{2,1,0:T(8,128)S(1)} %get-tuple-element.15, f32[1,16,1024]{2,1,0:T(8,128)S(1)} %get-tuple-element.14), kind=kOutput, calls=%fused_computation.33 | convolution fusion | flops 817922048 | bytes 12845056 | tf_op jit(solution)/shard_map/dot_general | solution.py:37
  94.2 14.0 %fusion.18 = f32[1,16,2048]{2,1,0:T(8,128)S(1)} fusion(f32[1024,1024]{1,0:T(8,128)} %get-tuple-element.19, f32[1024,1024]{1,0:T(8,128)} %get-tuple-element.21, f32[1024,1024]{1,0:T(8,128)} %get-tuple-element.20, f32[1,16,1024]{2,1,0:T(8,128)S(1)} %get-tuple-element.13, f32[1,16,1024]{2,1,0:T(8,128)S(1)} %get-tuple-element.12), kind=kOutput, calls=%fused_computation.32 | convolution fusion | flops 817922048 | bytes 12845056 | tf_op jit(solution)/shard_map/dot_general | solution.py:37
  108.2 0.5 fusion.54
  108.7 0.5 fusion.30
  109.2 0.5 fusion.52
  109.7 11.5 %stack.36 = bf16[1,1,16384]{0,1,2:T(2,128)(2,1)} reshape(bf16[16,1024]{1,0:T(8,128)(2,1)S(1)} %fusion.30) | data formatting | bytes 65536 | tf_op jit(solution)/shard_map/stack | solution.py:83
  121.2 0.5 fusion.31
  121.7 12.0 %stack.37 = bf16[1,1,16384]{0,1,2:T(2,128)(2,1)} reshape(bf16[16,1024]{1,0:T(8,128)(2,1)S(1)} %fusion.31) | data formatting | bytes 65536 | tf_op jit(solution)/shard_map/stack | solution.py:83
  133.6 25.2 %fusion.139 = bf16[16384,1,2]{2,1,0:T(2,128)(2,1)} fusion(bf16[1,1,16384]{0,1,2:T(2,128)(2,1)} %stack.37, bf16[1,1,16384]{0,1,2:T(2,128)(2,1)} %stack.36), kind=kLoop, calls=%fused_computation.177 | loop fusion | flops 131072 | bytes 131072
  158.8 0.5 broadcast.277
  159.4 90.8 %reduce = bf16[16384,2]{1,0:T(8,128)(2,1)} reduce(bf16[16384,1,2]{2,1,0:T(2,128)(2,1)} %fusion.139, bf16[]{:T(256)} %broadcast.277), dimensions={1}, to_apply=%fusion.139.reduce_sub_computation | reduce | bytes 131074
  250.2 7.2 %reshape.220 = bf16[16,2,1024]{2,1,0:T(2,128)(2,1)S(1)} reshape(bf16[16384,2]{1,0:T(8,128)(2,1)} %reduce) | data formatting | bytes 131072
  257.3 20.0 %all_to_all.21 = bf16[16,2,1024]{2,1,0:T(2,128)(2,1)S(1)} all-to-all(bf16[16,2,1024]{2,1,0:T(2,128)(2,1)S(1)} %reshape.220), channel_id=1, replica_groups=mesh['src'=16,'rcv'=16] {'rcv'}, dimensions={0} | all-to-all | bytes 131072 | tf_op jit(solution)/shard_map/all_to_all | solution.py:90
  277.3 11.9 %reshape.221 = bf16[16384,1,2]{2,1,0:T(2,128)(2,1)} reshape(bf16[16,2,1024]{2,1,0:T(2,128)(2,1)S(1)} %all_to_all.21) | data formatting | bytes 131072
  289.2 15.4 %copy.42 = bf16[2,1,16384]{2,0,1:T(2,128)(2,1)S(1)} copy(bf16[2,1,16384]{0,1,2:T(2,128)(2,1)} %bitcast.85) | data formatting | bytes 131072 | tf_op jit(solution)/shard_map/all_to_all | solution.py:90
  304.6 0.7 copy.62
  305.3 0.2 all-gather.8.cloned.1.call-start
  305.5 1.3 slice_bitcast_fusion.5
  306.8 26.9 %all-gather.6.cloned.1.call-done = bf16[2,256,1024]{2,1,0:T(8,128)(2,1)} async-done(((bf16[2,16,1024]{2,1,0:T(8,128)(2,1)}), bf16[2,256,1024]{2,1,0:T(8,128)(2,1)}) %all-gather.6.cloned.1.call-update) | async-done | bytes 1048592 | tf_op jit(solution)/shard_map/all_gather | solution.py:122
  333.7 1.3 slice_bitcast_fusion.2
  335.0 1.1 fusion.137
  336.1 2.4 fusion.32
  338.5 2.4 multiply_bitcast_fusion.3
  340.9 3.0 fusion.10
  343.9 6.2 %copy.43 = bf16[2,1024,1024]{1,2,0:T(8,128)(2,1)} copy(bf16[2,1024,1024]{2,1,0:T(8,128)(2,1)} %fusion.10) | data formatting | bytes 8388608 | tf_op jit(solution)/shard_map/convert_element_type | solution.py:131
  350.1 1.1 slice.99
  351.2 0.7 copy.63
  351.9 79.3 %all-gather.8.cloned.1.call-done = bf16[2,256,1024]{2,1,0:T(8,128)(2,1)} async-done(((bf16[2,16,1024]{2,1,0:T(8,128)(2,1)}), bf16[2,256,1024]{2,1,0:T(8,128)(2,1)}) %all-gather.8.cloned.1.call-update) | async-done | bytes 1048592 | tf_op jit(solution)/shard_map/all_gather | solution.py:115
  431.3 1.3 slice_bitcast_fusion.1
  432.5 2.4 fusion.36
  435.0 2.4 multiply_bitcast_fusion.1
  437.4 3.0 fusion.11
  (15 shorter events, 0.1 us)
Async XLA Ops:
  9.0 69.8 %all-to-all-start = ((bf16[2,16,1024]{2,0,1:T(2,128)(2,1)}), bf16[2,16,1024]{2,0,1:T(2,128)(2,1)S(1)}, u32[]{:S(2)}, u32[]{:S(2)}) async-start(bf16[2,16,1024]{2,0,1:T(2,128)(2,1)} %bitcast.83), calls=%async_computation | async-start | bytes 131072 | tf_op jit(solution)/shard_map/all_to_all | solution.py:88
  20.1 285.5 %all-gather.4.cloned.1.call-start = ((), (), s32[]{:S(2)}) async-start(), calls=%async_computation.2 | async-start | bytes 1114112 | tf_op jit(solution)/shard_map/all_gather | solution.py:115
  28.1 305.6 %all-gather.6.cloned.1.call-start = ((), (), s32[]{:S(2)}) async-start(), calls=%async_computation.3 | async-start | bytes 1114112 | tf_op jit(solution)/shard_map/all_gather | solution.py:122
  80.3 13.9 %copy-start.2 = (f32[16,1024]{1,0:T(8,128)S(1)}, f32[16,1024]{1,0:T(8,128)}, u32[]{:S(2)}) copy-start(f32[16,1024]{1,0:T(8,128)} %param.4) | copy-start | bytes 196612
  289.2 16.3 %copy-start.3 = (f32[1024]{0:T(1024)S(1)}, f32[1024]{0:T(1024)}, u32[]{:S(2)}) copy-start(f32[1024]{0:T(1024)} %param.5) | copy-start | bytes 12292
  305.3 126.0 %all-gather.8.cloned.1.call-start = ((), (), s32[]{:S(2)}) async-start(), calls=%async_computation.4 | async-start | bytes 1114112 | tf_op jit(solution)/shard_map/all_gather | solution.py:115
  338.5 2.5 copy-start
  434.9 2.5 copy-start.1
Sparse Core Ops, SparseCore 0:
  28.2 80.2 all-gather.3
  305.4 28.2 all-gather.5
  352.0 79.1 all-gather.7
where the time goes:
time: 452 us; the launch traced here: 447 us
  other arithmetic  179 us (40%)
  waiting for transfers between devices  106 us (23%)
  local copies, waits for them, and re-layouts  80.7 us (18%)
  matrix products  35.9 us (8%)
  blocking collectives  20 us (4%)
  between operations  14.2 us (3%)
  starting transfers between devices  11.3 us (2%)
    unnamed x2, other arithmetic  116 us
    all_gather x2, waiting for transfers between devices, per_device(): left_panel = lax.all_gather(left_local, 'rcv', axis=1, tiled=True)  79.4 us
    dot_general x2, matrix products, long_transform(): jnp.dot(joined.reshape(-1, 2 * length), long_table(length, orient), preci...  27.9 us
    unnamed x15, local copies, waits for them, and re-layouts  27.8 us
    all_gather x1, waiting for transfers between devices, per_device(): lax.all_gather(filtered, 'src', axis=1, tiled=True)  26.9 us
    another operation x2, local copies, waits for them, and re-layouts, filter_rows(): returned = jnp.stack([real_part * inverse_scale, imag_part * inverse_scale])  23.4 us
    all_to_all x1, blocking collectives, through_rows(): lax.all_to_all(returned, 'rcv', split_axis=2, concat_axis=1, tiled=True)  20 us
    mul x1, other arithmetic, long_table(): sine_part = orient * jnp.sin(angles)  17.6 us
  transfers between devices with their start and end apart: 4, of which 2 were waited for; matrix products, arithmetic and copies ran while one was open for 60% of the time, Pallas kernels for 0%

commit v1 on v0

--- a/solution.py
+++ b/solution.py
@@ -119,7 +119,11 @@
 
         zeros_init = jnp.zeros((row_total, 2 * col_total), jnp.float32)
         product_sum = accumulate(
-            zeros_init, lax.all_gather(filtered, "src", axis=1, tiled=True), jnp.int32(0)
+            zeros_init,
+            jnp.concatenate(
+                lax.all_to_all(jnp.stack([filtered] * lax.axis_size("src")), "src", 0, 0), axis=1
+            ),
+            jnp.int32(0),
         )
         pred_real = product_sum[:, :col_total]
         pred_imag = product_sum[:, col_total:]

time: 452 us -> 437 us (0.967)
  waiting for transfers between devices: 106 us -> 87.7 us
  starting transfers between devices: 11.3 us -> 16.2 us
    all_gather x1 -> x0, waiting for transfers between devices: 26.9 us -> none  [per_device(): lax.all_gather(filtered, 'src', axis=1, tiled=True)]
    all_to_all x0 -> x1, waiting for transfers between devices: none -> 13.3 us  [per_device(): lax.all_to_all(jnp.stack([filtered] * lax.axis_size('src')), 'src', 0, 0)]
    all_to_all x0 -> x1, starting transfers between devices: none -> 5.12 us  [per_device(): lax.all_to_all(jnp.stack([filtered] * lax.axis_size('src')), 'src', 0, 0)]
    all_gather x2, waiting for transfers between devices: 79.4 us -> 74.4 us  [per_device(): left_panel = lax.all_gather(left_local, 'rcv', axis=1, tiled=True)]
  transfers between devices with their start and end apart: 4 -> 4, of which waited for: 2 -> 2; matrix products, arithmetic and copies ran while one was open for 60% -> 61% of each run, Pallas kernels for 0% -> 0%
where the time goes in v1:
time: 437 us; the launch traced here: 432 us
  other arithmetic  178 us (41%)
  waiting for transfers between devices  87.7 us (20%)
  local copies, waits for them, and re-layouts  80 us (18%)
  matrix products  35.9 us (8%)
  blocking collectives  20 us (5%)
  starting transfers between devices  16.2 us (4%)
  between operations  14.5 us (3%)
    unnamed x2, other arithmetic  116 us
    all_gather x2, waiting for transfers between devices, per_device(): left_panel = lax.all_gather(left_local, 'rcv', axis=1, tiled=True)  74.4 us
    dot_general x2, matrix products, long_transform(): jnp.dot(joined.reshape(-1, 2 * length), long_table(length, orient), preci...  27.9 us
    unnamed x15, local copies, waits for them, and re-layouts  27.1 us
    another operation x2, local copies, waits for them, and re-layouts, filter_rows(): returned = jnp.stack([real_part * inverse_scale, imag_part * inverse_scale])  23.4 us
    all_to_all x1, blocking collectives, through_rows(): lax.all_to_all(returned, 'rcv', split_axis=2, concat_axis=1, tiled=True)  20 us
    mul x1, other arithmetic, long_table(): sine_part = orient * jnp.sin(angles)  17.6 us
    sin x1, other arithmetic, long_table(): sine_part = orient * jnp.sin(angles)  16.7 us
  transfers between devices with their start and end apart: 4, of which 2 were waited for; matrix products, arithmetic and copies ran while one was open for 61% of the time, Pallas kernels for 0%

profile of v1, /device:TPU:8, one launch (start us, length us, event | category | flops | bytes accessed | tf_op | source)
XLA Modules:
  0.0 432.0 jit_solution(10069409558429624840)
XLA Ops:
  7.2 1.1 slice.90
  8.3 0.7 copy.65
  9.0 11.0 %all-to-all-start = ((bf16[2,16,1024]{2,0,1:T(2,128)(2,1)}), bf16[2,16,1024]{2,0,1:T(2,128)(2,1)S(1)}, u32[]{:S(2)}, u32[]{:S(2)}) async-start(bf16[2,16,1024]{2,0,1:T(2,128)(2,1)} %bitcast.81), calls=%async_computation | async-start | bytes 131072 | tf_op jit(solution)/shard_map/all_to_all | solution.py:88
  20.0 0.0 all-gather.3.cloned.1.call-start
  20.1 6.2 %copy.36 = bf16[2,1024,1024]{1,2,0:T(8,128)(2,1)} copy(bf16[2,1024,1024]{2,1,0:T(8,128)(2,1)} %param.3) | data formatting | bytes 8388608 | tf_op args[0]
  26.3 1.1 slice.87
  27.4 0.6 copy.64
  28.1 17.6 %broadcast_multiply_fusion = (f32[1024,1024]{1,0:T(8,128)}, f32[1024,1024]{1,0:T(8,128)}) fusion(), kind=kLoop, calls=%fused_computation.35 | loop fusion | flops 15728640 | bytes 8388608 | tf_op jit(solution)/shard_map/mul | solution.py:28
  45.7 16.3 %fusion.27 = f32[1024,1024]{1,0:T(8,128)} fusion(), kind=kLoop, calls=%fused_computation.39 | loop fusion | flops 16777216 | bytes 4194304 | tf_op jit(solution)/shard_map/neg | solution.py:30
  62.1 16.7 %fusion.24 = (f32[1024,1024]{1,0:T(8,128)}, f32[1024,1024]{1,0:T(8,128)}) fusion(), kind=kLoop, calls=%fused_computation.36 | loop fusion | flops 15728640 | bytes 8388608 | tf_op jit(solution)/shard_map/sin | solution.py:28
  78.8 0.1 fusion.138
  78.9 0.3 fusion.65
  79.2 0.3 fusion.66
  79.5 0.3 convolution_add_fusion.1
  79.7 0.5 subtract_bitcast_fusion
  80.2 13.8 %fusion.21 = f32[1,16,2048]{2,1,0:T(8,128)S(1)} fusion(f32[1024,1024]{1,0:T(8,128)} %get-tuple-element.19, f32[1024,1024]{1,0:T(8,128)} %fusion.27, f32[1024,1024]{1,0:T(8,128)} %get-tuple-element.18, f32[1,16,1024]{2,1,0:T(8,128)S(1)} %get-tuple-element.15, f32[1,16,1024]{2,1,0:T(8,128)S(1)} %get-tuple-element.14), kind=kOutput, calls=%fused_computation.33 | convolution fusion | flops 817922048 | bytes 12845056 | tf_op jit(solution)/shard_map/dot_general | solution.py:37
  94.1 14.0 %fusion.18 = f32[1,16,2048]{2,1,0:T(8,128)S(1)} fusion(f32[1024,1024]{1,0:T(8,128)} %get-tuple-element.19, f32[1024,1024]{1,0:T(8,128)} %get-tuple-element.21, f32[1024,1024]{1,0:T(8,128)} %get-tuple-element.20, f32[1,16,1024]{2,1,0:T(8,128)S(1)} %get-tuple-element.13, f32[1,16,1024]{2,1,0:T(8,128)S(1)} %get-tuple-element.12), kind=kOutput, calls=%fused_computation.32 | convolution fusion | flops 817922048 | bytes 12845056 | tf_op jit(solution)/shard_map/dot_general | solution.py:37
  108.1 0.5 fusion.54
  108.6 0.5 fusion.52
  109.1 0.5 fusion.30
  109.6 11.5 %stack.33 = bf16[1,1,16384]{0,1,2:T(2,128)(2,1)} reshape(bf16[16,1024]{1,0:T(8,128)(2,1)S(1)} %fusion.30) | data formatting | bytes 65536 | tf_op jit(solution)/shard_map/stack | solution.py:83
  121.1 0.5 fusion.31
  121.6 11.9 %stack.34 = bf16[1,1,16384]{0,1,2:T(2,128)(2,1)} reshape(bf16[16,1024]{1,0:T(8,128)(2,1)S(1)} %fusion.31) | data formatting | bytes 65536 | tf_op jit(solution)/shard_map/stack | solution.py:83
  133.5 25.2 %fusion.139 = bf16[16384,1,2]{2,1,0:T(2,128)(2,1)} fusion(bf16[1,1,16384]{0,1,2:T(2,128)(2,1)} %stack.34, bf16[1,1,16384]{0,1,2:T(2,128)(2,1)} %stack.33), kind=kLoop, calls=%fused_computation.176 | loop fusion | flops 131072 | bytes 131072
  158.8 0.5 broadcast.278
  159.3 90.8 %reduce = bf16[16384,2]{1,0:T(8,128)(2,1)} reduce(bf16[16384,1,2]{2,1,0:T(2,128)(2,1)} %fusion.139, bf16[]{:T(256)} %broadcast.278), dimensions={1}, to_apply=%fusion.139.reduce_sub_computation | reduce | bytes 131074
  250.1 7.2 %reshape.234 = bf16[16,2,1024]{2,1,0:T(2,128)(2,1)S(1)} reshape(bf16[16384,2]{1,0:T(8,128)(2,1)} %reduce) | data formatting | bytes 131072
  257.3 20.0 %all_to_all.24 = bf16[16,2,1024]{2,1,0:T(2,128)(2,1)S(1)} all-to-all(bf16[16,2,1024]{2,1,0:T(2,128)(2,1)S(1)} %reshape.234), channel_id=1, replica_groups=mesh['src'=16,'rcv'=16] {'rcv'}, dimensions={0} | all-to-all | bytes 131072 | tf_op jit(solution)/shard_map/all_to_all | solution.py:90
  277.2 11.9 %reshape.235 = bf16[16384,1,2]{2,1,0:T(2,128)(2,1)} reshape(bf16[16,2,1024]{2,1,0:T(2,128)(2,1)S(1)} %all_to_all.24) | data formatting | bytes 131072
  289.1 15.4 %copy.42 = bf16[2,1,16384]{2,0,1:T(2,128)(2,1)S(1)} copy(bf16[2,1,16384]{0,1,2:T(2,128)(2,1)} %bitcast.83) | data formatting | bytes 131072 | tf_op jit(solution)/shard_map/all_to_all | solution.py:90
  304.5 1.1 stack.26
  305.6 5.1 %all-to-all-start.2 = ((bf16[16,2,16,1024]{3,2,1,0:T(8,128)(2,1)}), bf16[16,2,16,1024]{3,2,1,0:T(8,128)(2,1)S(1)}, u32[]{:S(2)}, u32[]{:S(2)}) async-start(bf16[16,2,16,1024]{3,2,1,0:T(8,128)(2,1)} %stack.26), calls=%async_computation.2 | async-start | bytes 2097152 | tf_op jit(solution)/shard_map/all_to_all | solution.py:124
  310.7 0.0 all-gather.5.cloned.1.call-start
  310.8 13.3 %all-to-all-done.2 = bf16[16,2,16,1024]{3,2,1,0:T(8,128)(2,1)S(1)} async-done(((bf16[16,2,16,1024]{3,2,1,0:T(8,128)(2,1)}), bf16[16,2,16,1024]{3,2,1,0:T(8,128)(2,1)S(1)}, u32[]{:S(2)}, u32[]{:S(2)}) %all-to-all-start.2) | async-done | bytes 1048608 | tf_op jit(solution)/shard_map/all_to_all | solution.py:124
  324.1 0.1 fusion.137
  324.2 0.1 bitcast_negate_fusion
  324.4 1.3 slice_bitcast_fusion.3
  325.6 2.4 fusion.32
  328.0 2.4 multiply_bitcast_fusion.3
  330.5 3.0 fusion.10
  333.5 6.2 %copy.43 = bf16[2,1024,1024]{1,2,0:T(8,128)(2,1)} copy(bf16[2,1024,1024]{2,1,0:T(8,128)(2,1)} %fusion.10) | data formatting | bytes 8388608 | tf_op jit(solution)/shard_map/convert_element_type | solution.py:135
  339.7 1.1 slice.101
  340.8 0.7 copy.63
  341.5 74.4 %all-gather.5.cloned.1.call-done = bf16[2,256,1024]{2,1,0:T(8,128)(2,1)} async-done(((bf16[2,16,1024]{2,1,0:T(8,128)(2,1)}), bf16[2,256,1024]{2,1,0:T(8,128)(2,1)}) %all-gather.5.cloned.1.call-update) | async-done | bytes 1048592 | tf_op jit(solution)/shard_map/all_gather | solution.py:115
  415.9 1.3 slice_bitcast_fusion.1
  417.1 2.4 fusion.36
  419.5 2.4 multiply_bitcast_fusion.1
  422.0 3.0 fusion.11
  (15 shorter events, 0.1 us)
Async XLA Ops:
  9.0 69.8 %all-to-all-start = ((bf16[2,16,1024]{2,0,1:T(2,128)(2,1)}), bf16[2,16,1024]{2,0,1:T(2,128)(2,1)S(1)}, u32[]{:S(2)}, u32[]{:S(2)}) async-start(bf16[2,16,1024]{2,0,1:T(2,128)(2,1)} %bitcast.81), calls=%async_computation | async-start | bytes 131072 | tf_op jit(solution)/shard_map/all_to_all | solution.py:88
  20.0 304.3 %all-gather.3.cloned.1.call-start = ((), (), s32[]{:S(2)}) async-start(), calls=%async_computation.3 | async-start | bytes 1114112 | tf_op jit(solution)/shard_map/all_gather | solution.py:115
  80.2 13.9 %copy-start.2 = (f32[16,1024]{1,0:T(8,128)S(1)}, f32[16,1024]{1,0:T(8,128)}, u32[]{:S(2)}) copy-start(f32[16,1024]{1,0:T(8,128)} %param.4) | copy-start | bytes 196612
  289.1 21.7 %copy-start.3 = (f32[1024]{0:T(1024)S(1)}, f32[1024]{0:T(1024)}, u32[]{:S(2)}) copy-start(f32[1024]{0:T(1024)} %param.5) | copy-start | bytes 12292
  305.6 18.5 %all-to-all-start.2 = ((bf16[16,2,16,1024]{3,2,1,0:T(8,128)(2,1)}), bf16[16,2,16,1024]{3,2,1,0:T(8,128)(2,1)S(1)}, u32[]{:S(2)}, u32[]{:S(2)}) async-start(bf16[16,2,16,1024]{3,2,1,0:T(8,128)(2,1)} %stack.26), calls=%async_computation.2 | async-start | bytes 2097152 | tf_op jit(solution)/shard_map/all_to_all | solution.py:124
  310.7 105.1 %all-gather.5.cloned.1.call-start = ((), (), s32[]{:S(2)}) async-start(), calls=%async_computation.4 | async-start | bytes 1114112 | tf_op jit(solution)/shard_map/all_gather | solution.py:115
  328.0 2.5 copy-start
  419.5 2.5 copy-start.1
Sparse Core Ops, SparseCore 0:
  28.2 80.2 all-gather.2
  341.6 74.1 all-gather.4
